TPU v7x, 32 devices: a whole 2x2x4 slice. The times are simulated.
32 devices in a mesh: rep: 2 (over core), mp: 16 (over z, y, x).
Axes of the slice: x: 2, y: 2, z: 4, core: 2. Of those that a mesh axis runs over, the one named last changes fastest.
Arguments:
- lookup_block: int32 [2, 2048, 16, 4], P(None, ('rep', 'mp')), may hold values from 0 to 9
- lookup_offset: int32 [2, 2048, 16, 4], P(None, ('rep', 'mp')), may hold values from 0 to 63
- interaction_grad: bfloat16 [2, 2048, 16, 16], P(None, ('rep', 'mp')), may hold values from -4 to 4
- table: bfloat16 [49152, 256], P('mp'), may hold values from -0.3125 to 0.3125
- adagrad_state: float32 [49152], P('mp'), may hold values from 0.05 to 2
- touched_blocks: int32 [16, 10], P('mp'), may hold values from 0 to 47, as said below
- dither: int32 [16, 640, 256], P('mp'), may hold values from 0 to 32767
Outputs:
- new_table: bfloat16 [49152, 256], P('mp')
- new_state: float32 [49152], P('mp')
Inputs may be any that keep to these rules, and one draw needn't show every extreme that they name: `touched_blocks`: each row names 10 different row blocks.
All inputs are finite; a program needn't handle non-finite values.
Results may differ from a plain program's by a relative error of at most 0.00055.
The roundings to bfloat16 on the way count: a program that leaves them out, or rounds other values in their place, can miss the bound.
Values may be sent and summed in bfloat16 or wider, within the bound.
A program may use at most 128 MiB of HBM per device.

v0:
```python
import jax
import jax.numpy as jnp
from jax import lax
from jax.sharding import PartitionSpec as P

BLOCK = 64
LEARN_RATE = 0.1
POOL_DECAY = 0.5
DITHER_UNIT = 2.0 ** (-15)
SMALLEST = 2.0 ** (-14)


def dither_round(weights, dither_bits):
    magnitude = jnp.maximum(jnp.abs(weights), SMALLEST)
    spacing = jnp.exp2(jnp.floor(jnp.log2(magnitude)) - 7.0)
    grid_level = jnp.floor(weights / spacing + dither_bits.astype(jnp.float32) * DITHER_UNIT)
    return (grid_level * spacing).astype(jnp.bfloat16)


def adagrad_rows(slab_rows, grad_rows, state_rows, dither_bits):
    state_next = state_rows + jnp.mean(grad_rows * grad_rows, axis=-1)
    moved = (
        slab_rows.astype(jnp.float32)
        - LEARN_RATE * grad_rows / (jnp.sqrt(state_next) + 1e-08)[:, None]
    )
    return (dither_round(moved, dither_bits), state_next)


def hit_counts(lookup_rows, slab_size):
    column = lax.broadcasted_iota(jnp.int32, (1, slab_size), 1)
    counted = jnp.zeros((lookup_rows.shape[0], slab_size), jnp.bfloat16)
    for lookup in range(lookup_rows.shape[1]):
        counted = counted + (lookup_rows[:, lookup : lookup + 1] == column).astype(jnp.bfloat16)
    return counted


def pairwise(pooled_rows, cotangent):
    forward = jnp.einsum("bfg,bge->bfe", cotangent, pooled_rows, preferred_element_type=jnp.float32)
    backward = jnp.einsum(
        "bgf,bge->bfe", cotangent, pooled_rows, preferred_element_type=jnp.float32
    )
    return (forward + backward + POOL_DECAY * pooled_rows.astype(jnp.float32)).astype(jnp.bfloat16)


def per_device(
    lookup_block, lookup_offset, interaction_grad, table, adagrad_state, touched_blocks, dither
):
    micro_count, sample_count, feature_count, bag_count = lookup_block.shape
    groups = lax.axis_size("mp")
    row_count, emb_width = table.shape
    touch_count = touched_blocks.shape[1]
    slab_size = touch_count * BLOCK
    owner_samples = groups * sample_count
    lookup_rows = lookup_block * BLOCK + lookup_offset
    owner_rows = lax.all_to_all(lookup_rows, "mp", split_axis=2, concat_axis=1, tiled=True)
    owner_rows = owner_rows.reshape(micro_count, owner_samples, bag_count)
    table_blocks = table.reshape(row_count // BLOCK, BLOCK, emb_width)
    slab_table = table_blocks[touched_blocks[0]].reshape(slab_size, emb_width)
    counted = [hit_counts(owner_rows[micro_index], slab_size) for micro_index in range(micro_count)]
    pooled_rows = [
        jnp.dot(hits, slab_table, preferred_element_type=jnp.float32).astype(jnp.bfloat16)
        for hits in counted
    ]
    returned = []
    outgoing = jnp.stack(pooled_rows).reshape(micro_count, groups, sample_count, 1, emb_width)
    arrived = lax.all_to_all(outgoing, "mp", split_axis=1, concat_axis=3, tiled=True)
    sample_pooled = arrived.reshape(micro_count * sample_count, feature_count, emb_width)
    cot_rows = interaction_grad.reshape(micro_count * sample_count, feature_count, feature_count)
    grad_rows = pairwise(sample_pooled, cot_rows)
    grad_rows = grad_rows.reshape(micro_count, 1, sample_count, feature_count, emb_width)
    sent_back = lax.all_to_all(grad_rows, "mp", split_axis=3, concat_axis=1, tiled=True)
    sent_back = sent_back.reshape(micro_count, owner_samples, emb_width)
    returned = [sent_back[micro_index] for micro_index in range(micro_count)]
    slab_grad = jnp.zeros((slab_size, emb_width), jnp.float32)
    for micro_index in range(micro_count):
        slab_grad = slab_grad + jnp.einsum(
            "sr,se->re",
            counted[micro_index],
            returned[micro_index],
            preferred_element_type=jnp.float32,
        )
    state_slab = adagrad_state.reshape(row_count // BLOCK, BLOCK)[touched_blocks[0]].reshape(
        slab_size
    )
    summed_grad = lax.psum(slab_grad, "rep")
    new_rows, state_next = adagrad_rows(slab_table, summed_grad, state_slab, dither[0])
    updated_blocks = table_blocks.at[touched_blocks[0]].set(
        new_rows.reshape(touch_count, BLOCK, emb_width)
    )
    state_blocks = adagrad_state.reshape(row_count // BLOCK, BLOCK)
    updated_state = state_blocks.at[touched_blocks[0]].set(state_next.reshape(touch_count, BLOCK))
    return (updated_blocks.reshape(row_count, emb_width), updated_state.reshape(row_count))


def solution(mesh):
    return jax.shard_map(
        per_device,
        mesh=mesh,
        in_specs=(
            P(None, ("rep", "mp"), None, None),
            P(None, ("rep", "mp"), None, None),
            P(None, ("rep", "mp"), None, None),
            P("mp", None),
            P("mp"),
            P("mp", None),
            P("mp", None, None),
        ),
        out_specs=(P("mp", None), P("mp")),
        check_vma=False,
    )
```

profile of v0, /device:TPU:0, one launch (start us, length us, event | category | flops | bytes accessed | tf_op | source)
XLA Modules:
  0.0 124.7 jit_solution(17753280693400444190)
XLA Ops:
  7.2 1.5 %copy.46 = bf16[3072,256]{1,0:T(8,128)(2,1)S(1)} copy(bf16[3072,256]{1,0:T(8,128)(2,1)} %param.10) | data formatting | bytes 3145728
  8.7 0.7 reshape.142
  9.4 8.3 %all-to-all-start = ((s32[16,1,512]{2,1,0:T(1,128)}), s32[16,1,512]{2,1,0:T(1,128)S(1)}, u32[]{:S(2)}, u32[]{:S(2)}) async-start(s32[16,1,512]{2,1,0:T(1,128)} %reshape.142), calls=%async_computation | async-start | bytes 65536 | tf_op jit(solution)/shard_map/all_to_all | solution.py:55
  17.8 0.6 gather_fusion
  18.4 6.8 %all-to-all-done = s32[16,1,512]{2,1,0:T(1,128)S(1)} async-done(((s32[16,1,512]{2,1,0:T(1,128)}), s32[16,1,512]{2,1,0:T(1,128)S(1)}, u32[]{:S(2)}, u32[]{:S(2)}) %all-to-all-start) | async-done | bytes 32800 | tf_op jit(solution)/shard_map/all_to_all | solution.py:55
  25.2 0.5 broadcast.49
  25.7 0.7 reduce
  26.4 0.1 reshape.143
  26.5 0.1 squeeze.20
  26.7 0.1 squeeze.21
  26.8 1.8 %convolution_convert_fusion.1 = bf16[1024,256]{1,0:T(8,128)(2,1)S(1)} fusion(bf16[640,256]{1,0:T(8,128)(2,1)S(1)} %bitcast.83, s32[1024]{0:T(1024)S(1)} %bitcast.91, s32[1024]{0:T(1024)S(1)} %bitcast.93, s32[1024]{0:T(1024)S(1)} %bitcast.95, s32[1024]{0:T(1024)S(1)} %bitcast.89), kind=kOutput, calls=%fused_computation.29 | convolution fusion | flops 346292224 | bytes 868352 | tf_op jit(solution)/shard_map/dot_general | solution.py:61
  28.6 1.8 %convolution_convert_fusion = bf16[1024,256]{1,0:T(8,128)(2,1)S(1)} fusion(bf16[640,256]{1,0:T(8,128)(2,1)S(1)} %bitcast.84, s32[1024]{0:T(1024)S(1)} %bitcast.99, s32[1024]{0:T(1024)S(1)} %bitcast.101, s32[1024]{0:T(1024)S(1)} %bitcast.103, s32[1024]{0:T(1024)S(1)} %bitcast.97), kind=kOutput, calls=%fused_computation.28 | convolution fusion | flops 346292224 | bytes 868352 | tf_op jit(solution)/shard_map/dot_general | solution.py:61
  30.3 1.1 pad_maximum_fusion
  31.4 3.7 %all-to-all-start.1 = ((bf16[2,16,64,1,256]{4,2,3,0,1:T(8,128)(2,1)}), bf16[2,16,64,1,256]{4,2,3,0,1:T(8,128)(2,1)S(1)}, u32[]{:S(2)}, u32[]{:S(2)}) async-start(bf16[2,16,64,1,256]{4,2,3,0,1:T(8,128)(2,1)} %pad_maximum_fusion), calls=%async_computation.1 | async-start | bytes 2097152 | tf_op jit(solution)/shard_map/all_to_all | solution.py:66
  35.1 1.4 %copy.30 = bf16[2,64,16,16]{2,3,1,0:T(8,128)(2,1)S(1)} copy(bf16[2,64,16,16]{1,3,2,0:T(8,128)(2,1)} %param.9) | data formatting | bytes 131072 | tf_op jit(solution)/shard_map/reshape | solution.py:68
  36.5 21.7 %all-to-all-done.1 = bf16[2,16,64,1,256]{4,2,3,0,1:T(8,128)(2,1)S(1)} async-done(((bf16[2,16,64,1,256]{4,2,3,0,1:T(8,128)(2,1)}), bf16[2,16,64,1,256]{4,2,3,0,1:T(8,128)(2,1)S(1)}, u32[]{:S(2)}, u32[]{:S(2)}) %all-to-all-start.1) | async-done | bytes 1048608 | tf_op jit(solution)/shard_map/all_to_all | solution.py:66
  58.3 0.6 copy.24
  58.9 0.5 fusion.31
  59.3 0.5 fusion.8
  59.8 0.4 copy.28
  60.2 30.6 %all_to_all.45 = bf16[2,1,64,16,256]{4,2,0,1,3:T(8,128)(2,1)S(1)} all-to-all(bf16[2,1,64,16,256]{4,2,0,1,3:T(8,128)(2,1)S(1)} %copy.28), channel_id=1, replica_groups=mesh['rep'=2,'mp'=16] {'mp'}, dimensions={3} | all-to-all | bytes 2097152 | tf_op jit(solution)/shard_map/all_to_all | solution.py:71
  90.8 0.1 copy.41
  90.9 0.1 fusion.26
  91.0 1.7 %fusion.15 = f32[640,256]{1,0:T(8,128)S(1)} fusion(bf16[1024,256]{1,0:T(8,128)(2,1)S(1)} %bitcast.86, s32[1024]{0:T(1024)S(1)} %bitcast.92, s32[1024]{0:T(1024)S(1)} %bitcast.94, s32[1024]{0:T(1024)S(1)} %bitcast.96, s32[1024]{0:T(1024)S(1)} %bitcast.90), kind=kOutput, calls=%fused_computation.31 | convolution fusion | flops 346030080 | bytes 1196032 | tf_op jit(solution)/shard_map/sr,se->re/dot_general | solution.py:76
  92.8 2.5 %convolution_add_fusion = f32[640,256]{1,0:T(8,128)} fusion(f32[640,256]{1,0:T(8,128)S(1)} %fusion.15, bf16[1024,256]{1,0:T(8,128)(2,1)S(1)} %bitcast.85, s32[1024]{0:T(1024)S(1)} %bitcast.100, s32[1024]{0:T(1024)S(1)} %bitcast.102, s32[1024]{0:T(1024)S(1)} %bitcast.104, s32[1024]{0:T(1024)S(1)} %bitcast.98), kind=kOutput, calls=%fused_computation.30 | convolution fusion | flops 346193920 | bytes 1851392 | tf_op jit(solution)/shard_map/sr,se->re/dot_general | solution.py:76
  95.4 0.6 gather_fusion.1
  96.0 16.5 %all-reduce.2.cloned.1.call-done = f32[640,256]{1,0:T(8,128)} async-done(((f32[640,256]{1,0:T(8,128)}), f32[640,256]{1,0:T(8,128)}) %all-reduce.2.cloned.1.call-update) | async-done | bytes 655376 | tf_op jit(solution)/shard_map/psum | solution.py:85
  112.5 1.3 %multiply_reduce_fusion = f32[640]{0:T(1024)S(1)} fusion(f32[640,256]{1,0:T(8,128)} %all-reduce.2.cloned.1.call-done), kind=kLoop, calls=%fused_computation.38 | loop fusion | flops 327040 | bytes 657920 | tf_op jit(solution)/shard_map/reduce_sum | solution.py:21
  113.8 1.6 %fusion.22 = bf16[640,256]{1,0:T(8,128)(2,1)S(1)} fusion(s32[1,640,256]{2,1,0:T(8,128)S(1)} %copy-done.1, f32[640,256]{1,0:T(8,128)} %all-reduce.2.cloned.1.call-done, f32[640]{0:T(1024)S(1)} %get-tuple-element.15, bf16[10,64,256]{2,1,0:T(8,128)(2,1)S(1)} %gather_fusion), kind=kLoop, calls=%fused_computation.37 | loop fusion | flops 2785280 | bytes 1968640 | tf_op jit(solution)/shard_map/convert_element_type | solution.py:17
  115.4 1.0 scatter_fusion
  116.5 0.6 scatter_custom_fusion.1
  117.2 0.7 reshape.107
  (27 shorter events, 0.4 us)
Async XLA Ops:
  7.2 1.5 %copy-start.3 = (s32[2,64,16,4]{1,3,2,0:T(4,128)S(1)}, s32[2,64,16,4]{1,3,2,0:T(4,128)}, u32[]{:S(2)}) copy-start(s32[2,64,16,4]{1,3,2,0:T(4,128)} %param.7) | copy-start | bytes 98308
  7.2 1.5 %copy-start.2 = (s32[2,64,16,4]{1,3,2,0:T(4,128)S(1)}, s32[2,64,16,4]{1,3,2,0:T(4,128)}, u32[]{:S(2)}) copy-start(s32[2,64,16,4]{1,3,2,0:T(4,128)} %param.8) | copy-start | bytes 98308
  7.2 10.6 %copy-start.5 = (s32[1,10]{1,0:T(1,128)S(1)}, s32[1,10]{1,0:T(1,128)}, u32[]{:S(2)}) copy-start(s32[1,10]{1,0:T(1,128)} %param.12) | copy-start | bytes 124
  9.4 15.8 %all-to-all-start = ((s32[16,1,512]{2,1,0:T(1,128)}), s32[16,1,512]{2,1,0:T(1,128)S(1)}, u32[]{:S(2)}, u32[]{:S(2)}) async-start(s32[16,1,512]{2,1,0:T(1,128)} %reshape.142), calls=%async_computation | async-start | bytes 65536 | tf_op jit(solution)/shard_map/all_to_all | solution.py:55
  31.4 26.9 %all-to-all-start.1 = ((bf16[2,16,64,1,256]{4,2,3,0,1:T(8,128)(2,1)}), bf16[2,16,64,1,256]{4,2,3,0,1:T(8,128)(2,1)S(1)}, u32[]{:S(2)}, u32[]{:S(2)}) async-start(bf16[2,16,64,1,256]{4,2,3,0,1:T(8,128)(2,1)} %pad_maximum_fusion), calls=%async_computation.1 | async-start | bytes 2097152 | tf_op jit(solution)/shard_map/all_to_all | solution.py:66
  35.1 77.4 %all-reduce.2.cloned.1.call-start = ((), (), s32[]{:S(2)}) async-start(), calls=%async_computation.3 | async-start | bytes 1310720 | tf_op jit(solution)/shard_map/psum | solution.py:85
  92.7 2.5 %copy-start.4 = (f32[3072]{0:T(1024)S(1)}, f32[3072]{0:T(1024)}, u32[]{:S(2)}) copy-start(f32[3072]{0:T(1024)} %param.11) | copy-start | bytes 36868
  92.7 21.0 %copy-start.1 = (s32[1,640,256]{2,1,0:T(8,128)S(1)}, s32[1,640,256]{2,1,0:T(8,128)}, u32[]{:S(2)}) copy-start(s32[1,640,256]{2,1,0:T(8,128)} %param.13) | copy-start | bytes 1966084
  116.5 1.4 %copy-start = (bf16[48,64,256]{2,1,0:T(8,128)(2,1)}, bf16[48,64,256]{2,1,0:T(8,128)(2,1)S(1)}, u32[]{:S(2)}) copy-start(bf16[48,64,256]{2,1,0:T(8,128)(2,1)S(1)} %scatter_fusion) | copy-start | bytes 4718596
Sparse Core Ops, SparseCore 0:
  95.4 17.0 all-reduce.1
where the time goes:
time: 125 us
  waiting for transfers between devices  45 us (36%)
  blocking collectives  30.6 us (24%)
  between operations  14.3 us (11%)
  starting transfers between devices  12 us (10%)
  matrix products  8.71 us (7%)
  local copies, waits for them, and re-layouts  8.62 us (7%)
  other arithmetic  5.37 us (4%)
    all_to_all x1, blocking collectives, per_device(): lax.all_to_all(grad_rows, 'mp', split_axis=3, concat_axis=1, tiled=True)  30.6 us
    all_to_all x1, waiting for transfers between devices, per_device(): lax.all_to_all(outgoing, 'mp', split_axis=1, concat_axis=3, tiled=True)  21.7 us
    psum x1, waiting for transfers between devices, per_device(): summed_grad = lax.psum(slab_grad, 'rep')  16.5 us
    all_to_all x1, starting transfers between devices, per_device(): lax.all_to_all(lookup_rows, 'mp', split_axis=2, concat_axis=1, tiled=True)  8.34 us
    all_to_all x1, waiting for transfers between devices, per_device(): lax.all_to_all(lookup_rows, 'mp', split_axis=2, concat_axis=1, tiled=True)  6.79 us
    dot_general x2, matrix products, per_device(): jnp.einsum('sr,se->re', counted[micro_index], returned[micro_index], pref...  4.17 us
    all_to_all x1, starting transfers between devices, per_device(): lax.all_to_all(outgoing, 'mp', split_axis=1, concat_axis=3, tiled=True)  3.66 us
    dot_general x2, matrix products, per_device(): jnp.dot(hits, slab_table, preferred_element_type=jnp.float32)  3.58 us
  transfers between devices with their start and end apart: 3, of which 3 were waited for; matrix products, arithmetic and copies ran while one was open for 2% of the time, Pallas kernels for 0%

commit v1 on v0

--- a/solution.py
+++ b/solution.py
@@ -82,7 +82,8 @@
     state_slab = adagrad_state.reshape(row_count // BLOCK, BLOCK)[touched_blocks[0]].reshape(
         slab_size
     )
-    summed_grad = lax.psum(slab_grad, "rep")
+    blocks = lax.all_gather(slab_grad, "rep", axis=0, tiled=False)
+    summed_grad = blocks.sum(axis=0)
     new_rows, state_next = adagrad_rows(slab_table, summed_grad, state_slab, dither[0])
     updated_blocks = table_blocks.at[touched_blocks[0]].set(
         new_rows.reshape(touch_count, BLOCK, emb_width)

time: 125 us -> 118 us (0.944)
  waiting for transfers between devices: 45 us -> 36 us
  other arithmetic: 5.37 us -> 6.95 us
    psum x1 -> x0, waiting for transfers between devices: 16.5 us -> none  [per_device(): summed_grad = lax.psum(slab_grad, 'rep')]
    all_gather x0 -> x1, waiting for transfers between devices: none -> 6.53 us  [per_device(): blocks = lax.all_gather(slab_grad, 'rep', axis=0, tiled=False)]
    reduce_sum x0 -> x1, other arithmetic: none -> 1.47 us  [per_device(): summed_grad = blocks.sum(axis=0)]
    scatter x1, other arithmetic: 0.63 us -> 1.92 us  [per_device(): state_blocks.at[touched_blocks[0]]]
    unnamed x15 -> x23, local copies, waits for them, and re-layouts: 2.3 us -> 3.27 us
  transfers between devices with their start and end apart: 3 -> 3, of which waited for: 3 -> 3; matrix products, arithmetic and copies ran while one was open for 2% -> 1% of each run, Pallas kernels for 0% -> 0%
where the time goes in v1:
time: 118 us; the launch traced here: 117 us
  waiting for transfers between devices  36 us (31%)
  blocking collectives  30.6 us (26%)
  between operations  14.3 us (12%)
  starting transfers between devices  12 us (10%)
  matrix products  8.69 us (7%)
  local copies, waits for them, and re-layouts  8.68 us (7%)
  other arithmetic  6.95 us (6%)
    all_to_all x1, blocking collectives, per_device(): lax.all_to_all(grad_rows, 'mp', split_axis=3, concat_axis=1, tiled=True)  30.6 us
    all_to_all x1, waiting for transfers between devices, per_device(): lax.all_to_all(outgoing, 'mp', split_axis=1, concat_axis=3, tiled=True)  22.7 us
    all_to_all x1, starting transfers between devices, per_device(): lax.all_to_all(lookup_rows, 'mp', split_axis=2, concat_axis=1, tiled=True)  8.34 us
    all_to_all x1, waiting for transfers between devices, per_device(): lax.all_to_all(lookup_rows, 'mp', split_axis=2, concat_axis=1, tiled=True)  6.78 us
    all_gather x1, waiting for transfers between devices, per_device(): blocks = lax.all_gather(slab_grad, 'rep', axis=0, tiled=False)  6.53 us
    dot_general x2, matrix products, per_device(): jnp.einsum('sr,se->re', counted[micro_index], returned[micro_index], pref...  4.16 us
    all_to_all x1, starting transfers between devices, per_device(): lax.all_to_all(outgoing, 'mp', split_axis=1, concat_axis=3, tiled=True)  3.66 us
    dot_general x2, matrix products, per_device(): jnp.dot(hits, slab_table, preferred_element_type=jnp.float32)  3.58 us
  transfers between devices with their start and end apart: 3, of which 3 were waited for; matrix products, arithmetic and copies ran while one was open for 1% of the time, Pallas kernels for 0%

profile of v1, /device:TPU:0, one launch (start us, length us, event | category | flops | bytes accessed | tf_op | source)
XLA Modules:
  0.0 117.3 jit_solution(5608396328332559606)
XLA Ops:
  7.2 1.5 %copy.45 = bf16[3072,256]{1,0:T(8,128)(2,1)S(1)} copy(bf16[3072,256]{1,0:T(8,128)(2,1)} %param.10) | data formatting | bytes 3145728
  8.7 0.7 reshape.146
  9.4 8.3 %all-to-all-start = ((s32[16,1,512]{2,1,0:T(1,128)}), s32[16,1,512]{2,1,0:T(1,128)S(1)}, u32[]{:S(2)}, u32[]{:S(2)}) async-start(s32[16,1,512]{2,1,0:T(1,128)} %reshape.146), calls=%async_computation | async-start | bytes 65536 | tf_op jit(solution)/shard_map/all_to_all | solution.py:55
  17.8 0.6 gather_fusion
  18.4 6.8 %all-to-all-done = s32[16,1,512]{2,1,0:T(1,128)S(1)} async-done(((s32[16,1,512]{2,1,0:T(1,128)}), s32[16,1,512]{2,1,0:T(1,128)S(1)}, u32[]{:S(2)}, u32[]{:S(2)}) %all-to-all-start) | async-done | bytes 32800 | tf_op jit(solution)/shard_map/all_to_all | solution.py:55
  25.2 0.5 broadcast.59
  25.7 0.7 reduce
  26.8 1.8 %convolution_convert_fusion.1 = bf16[1024,256]{1,0:T(8,128)(2,1)S(1)} fusion(bf16[640,256]{1,0:T(8,128)(2,1)S(1)} %bitcast.78, s32[1024]{0:T(1024)S(1)} %bitcast.86, s32[1024]{0:T(1024)S(1)} %bitcast.88, s32[1024]{0:T(1024)S(1)} %bitcast.90, s32[1024]{0:T(1024)S(1)} %bitcast.84), kind=kOutput, calls=%fused_computation.29 | convolution fusion | flops 346292224 | bytes 868352 | tf_op jit(solution)/shard_map/dot_general | solution.py:61
  28.6 1.8 %convolution_convert_fusion = bf16[1024,256]{1,0:T(8,128)(2,1)S(1)} fusion(bf16[640,256]{1,0:T(8,128)(2,1)S(1)} %bitcast.79, s32[1024]{0:T(1024)S(1)} %bitcast.94, s32[1024]{0:T(1024)S(1)} %bitcast.96, s32[1024]{0:T(1024)S(1)} %bitcast.98, s32[1024]{0:T(1024)S(1)} %bitcast.92), kind=kOutput, calls=%fused_computation.28 | convolution fusion | flops 346292224 | bytes 868352 | tf_op jit(solution)/shard_map/dot_general | solution.py:61
  30.4 1.1 pad_maximum_fusion
  31.4 3.7 %all-to-all-start.1 = ((bf16[2,16,64,1,256]{4,2,3,0,1:T(8,128)(2,1)}), bf16[2,16,64,1,256]{4,2,3,0,1:T(8,128)(2,1)S(1)}, u32[]{:S(2)}, u32[]{:S(2)}) async-start(bf16[2,16,64,1,256]{4,2,3,0,1:T(8,128)(2,1)} %pad_maximum_fusion), calls=%async_computation.1 | async-start | bytes 2097152 | tf_op jit(solution)/shard_map/all_to_all | solution.py:66
  35.2 0.5 copy.30
  35.6 22.7 %all-to-all-done.1 = bf16[2,16,64,1,256]{4,2,3,0,1:T(8,128)(2,1)S(1)} async-done(((bf16[2,16,64,1,256]{4,2,3,0,1:T(8,128)(2,1)}), bf16[2,16,64,1,256]{4,2,3,0,1:T(8,128)(2,1)S(1)}, u32[]{:S(2)}, u32[]{:S(2)}) %all-to-all-start.1) | async-done | bytes 1048608 | tf_op jit(solution)/shard_map/all_to_all | solution.py:66
  58.3 0.6 copy.24
  58.9 0.5 fusion.28
  59.4 0.5 fusion.8
  59.8 0.4 copy.28
  60.2 30.6 %all_to_all.45 = bf16[2,1,64,16,256]{4,2,0,1,3:T(8,128)(2,1)S(1)} all-to-all(bf16[2,1,64,16,256]{4,2,0,1,3:T(8,128)(2,1)S(1)} %copy.28), channel_id=1, replica_groups=mesh['rep'=2,'mp'=16] {'mp'}, dimensions={3} | all-to-all | bytes 2097152 | tf_op jit(solution)/shard_map/all_to_all | solution.py:71
  90.8 0.1 copy.41
  91.0 0.1 fusion.23
  91.1 1.7 %fusion.15 = f32[640,256]{1,0:T(8,128)S(1)} fusion(bf16[1024,256]{1,0:T(8,128)(2,1)S(1)} %bitcast.81, s32[1024]{0:T(1024)S(1)} %bitcast.87, s32[1024]{0:T(1024)S(1)} %bitcast.89, s32[1024]{0:T(1024)S(1)} %bitcast.91, s32[1024]{0:T(1024)S(1)} %bitcast.85), kind=kOutput, calls=%fused_computation.31 | convolution fusion | flops 346030080 | bytes 1196032 | tf_op jit(solution)/shard_map/sr,se->re/dot_general | solution.py:76
  92.8 2.5 %convolution_add_fusion = f32[640,256]{1,0:T(8,128)} fusion(f32[640,256]{1,0:T(8,128)S(1)} %fusion.15, bf16[1024,256]{1,0:T(8,128)(2,1)S(1)} %bitcast.80, s32[1024]{0:T(1024)S(1)} %bitcast.95, s32[1024]{0:T(1024)S(1)} %bitcast.97, s32[1024]{0:T(1024)S(1)} %bitcast.99, s32[1024]{0:T(1024)S(1)} %bitcast.93), kind=kOutput, calls=%fused_computation.30 | convolution fusion | flops 346193920 | bytes 1851392 | tf_op jit(solution)/shard_map/sr,se->re/dot_general | solution.py:76
  95.4 0.6 copy-done.3
  96.0 0.6 gather_fusion.1
  96.6 6.5 %all-gather.3.cloned.1.call-done = f32[1280,256]{1,0:T(8,128)} async-done(((f32[640,256]{1,0:T(8,128)}), f32[1280,256]{1,0:T(8,128)}) %all-gather.3.cloned.1.call-update) | async-done | bytes 1310736 | tf_op jit(solution)/shard_map/all_gather | solution.py:85
  103.1 1.5 %reduce_sum.18 = f32[640,256]{1,0:T(8,128)S(1)} reduce(f32[2,640,256]{2,1,0:T(8,128)} %bitcast.77, f32[]{:T(128)} %constant.6.clone.1), dimensions={0}, to_apply=%region_0.0 | reduce | flops 163840 | bytes 1966084 | tf_op jit(solution)/shard_map/reduce_sum | solution.py:86
  104.6 0.2 multiply_reduce_fusion
  104.9 1.9 %scatter_custom_fusion.1 = f32[48,64]{1,0:T(8,128)} fusion(f32[48,64]{1,0:T(8,128)} %copy-done.3, s32[10]{0:T(128)S(1)} %fusion.22, f32[10,64]{1,0:T(8,128)S(1)} %gather_fusion.1, f32[10,64]{1,0:T(8,128)S(1)} %div.23), kind=kCustom, calls=%fused_computation.42 | custom fusion | flops 640 | bytes 28672 | tf_op jit(solution)/shard_map/scatter | solution.py:92
  106.8 1.5 %multiply_convert_fusion = bf16[10,64,256]{2,1,0:T(8,128)(2,1)S(1)} fusion(f32[10,64,256]{2,1,0:T(8,128)S(1)} %bitcast.75, f32[10,64,256]{2,1,0:T(8,128)S(1)} %bitcast.76, bf16[10,64,256]{2,1,0:T(8,128)(2,1)} %copy-done.1, f32[10,64]{1,0:T(8,128)S(1)} %sqrt_add_fusion), kind=kLoop, calls=%fused_computation.34 | loop fusion | flops 2293760 | bytes 1968640 | tf_op jit(solution)/shard_map/convert_element_type | solution.py:17
  108.3 1.0 scatter_fusion
  109.3 0.8 reshape.110
  110.1 0.4 copy-done
  (37 shorter events, 0.7 us)
Async XLA Ops:
  7.2 1.5 %copy-start.7 = (s32[2,64,16,4]{1,3,2,0:T(4,128)S(1)}, s32[2,64,16,4]{1,3,2,0:T(4,128)}, u32[]{:S(2)}) copy-start(s32[2,64,16,4]{1,3,2,0:T(4,128)} %param.7) | copy-start | bytes 98308
  7.2 1.5 %copy-start.6 = (s32[2,64,16,4]{1,3,2,0:T(4,128)S(1)}, s32[2,64,16,4]{1,3,2,0:T(4,128)}, u32[]{:S(2)}) copy-start(s32[2,64,16,4]{1,3,2,0:T(4,128)} %param.8) | copy-start | bytes 98308
  7.2 10.6 %copy-start.9 = (s32[1,10]{1,0:T(1,128)S(1)}, s32[1,10]{1,0:T(1,128)}, u32[]{:S(2)}) copy-start(s32[1,10]{1,0:T(1,128)} %param.12) | copy-start | bytes 124
  9.4 15.8 %all-to-all-start = ((s32[16,1,512]{2,1,0:T(1,128)}), s32[16,1,512]{2,1,0:T(1,128)S(1)}, u32[]{:S(2)}, u32[]{:S(2)}) async-start(s32[16,1,512]{2,1,0:T(1,128)} %reshape.146), calls=%async_computation | async-start | bytes 65536 | tf_op jit(solution)/shard_map/all_to_all | solution.py:55
  18.4 10.2 %copy-start.1 = (bf16[10,64,256]{2,1,0:T(8,128)(2,1)}, bf16[10,64,256]{2,1,0:T(8,128)(2,1)S(1)}, u32[]{:S(2)}) copy-start(bf16[10,64,256]{2,1,0:T(8,128)(2,1)S(1)} %gather_fusion) | copy-start | bytes 983044
  30.4 4.8 %copy-start.5 = (bf16[2,64,16,16]{1,3,2,0:T(8,128)(2,1)S(1)}, bf16[2,64,16,16]{1,3,2,0:T(8,128)(2,1)}, u32[]{:S(2)}) copy-start(bf16[2,64,16,16]{1,3,2,0:T(8,128)(2,1)} %param.9) | copy-start | bytes 196612
  31.4 26.9 %all-to-all-start.1 = ((bf16[2,16,64,1,256]{4,2,3,0,1:T(8,128)(2,1)}), bf16[2,16,64,1,256]{4,2,3,0,1:T(8,128)(2,1)S(1)}, u32[]{:S(2)}, u32[]{:S(2)}) async-start(bf16[2,16,64,1,256]{4,2,3,0,1:T(8,128)(2,1)} %pad_maximum_fusion), calls=%async_computation.1 | async-start | bytes 2097152 | tf_op jit(solution)/shard_map/all_to_all | solution.py:66
  35.1 68.0 %all-gather.3.cloned.1.call-start = ((), (), s32[]{:S(2)}) async-start(), calls=%async_computation.3 | async-start | bytes 1966080 | tf_op jit(solution)/shard_map/all_gather | solution.py:85
  92.8 2.5 %copy-start.8 = (f32[3072]{0:T(1024)S(1)}, f32[3072]{0:T(1024)}, u32[]{:S(2)}) copy-start(f32[3072]{0:T(1024)} %param.11) | copy-start | bytes 36868
  92.8 3.8 %copy-start.2 = (s32[1,640,256]{2,1,0:T(8,128)S(1)}, s32[1,640,256]{2,1,0:T(8,128)}, u32[]{:S(2)}) copy-start(s32[1,640,256]{2,1,0:T(8,128)} %param.13) | copy-start | bytes 1966084
  95.4 0.6 copy-start.3
  106.8 2.5 %copy-start.4 = (f32[48,64]{1,0:T(8,128)S(1)}, f32[48,64]{1,0:T(8,128)}, u32[]{:S(2)}) copy-start(f32[48,64]{1,0:T(8,128)} %scatter_custom_fusion.1) | copy-start | bytes 36868
  109.3 1.1 copy-start
Sparse Core Ops, SparseCore 0:
  95.4 7.6 all-gather.2
